TPU v7x, 32 devices: a whole 2x2x4 slice. The times are simulated.
32 devices in a mesh: snap: 16 (over z, y, x), vert: 2 (over core).
Axes of the slice: x: 2, y: 2, z: 4, core: 2. Of those that a mesh axis runs over, the one named last changes fastest.
Arguments:
- features: bfloat16 [32, 2048, 128], P('snap', 'vert'), may hold values from -6 to 6
- tile_cols: int32 [32, 16, 8], P('snap', 'vert'), may hold values from 0 to 15
- tile_weights: int32 [32, 16, 8, 128, 128], P('snap', 'vert'), may hold values from 0 to 3
- graph_gain: float32 [2, 128], replicated, may hold values from 0.5 to 1.5
- graph_up: bfloat16 [2, 128, 512], replicated, may hold values from -0.5 to 0.5
- graph_down: bfloat16 [2, 512, 128], replicated, may hold values from -0.25 to 0.25
- lag_mix: float32 [2, 8, 128], replicated, may hold values from -2 to 2
- time_gain: float32 [2, 128], replicated, may hold values from 0.5 to 1.5
- time_up: bfloat16 [2, 128, 1024], replicated, may hold values from -0.5 to 0.5
- time_down: bfloat16 [2, 1024, 128], replicated, may hold values from -0.1875 to 0.1875
Outputs:
- result: bfloat16 [32, 2048, 128], P('snap', 'vert')
All inputs are finite; a program needn't handle non-finite values.
Results may differ from a plain program's by a relative error of at most 0.0085.
Values may be sent and summed in bfloat16 or wider, within the bound.
A program may use at most 64 MiB of HBM per device.

v0:
```python
import functools

import jax
import jax.numpy as jnp
from jax import lax
from jax.experimental import pallas as pl
from jax.experimental.pallas import tpu as pltpu
from jax.sharding import PartitionSpec as P

eps = 1e-06
MESH = pl.DeviceIdType.MESH


def normalise(rows, gain_row):
    scale = lax.rsqrt(jnp.mean(rows * rows, axis=-1, keepdims=True) + eps)
    return (rows * scale * gain_row).astype(jnp.bfloat16)


def mlp(normed, up_weight, down_weight):
    hidden = jnp.dot(normed, up_weight, preferred_element_type=jnp.float32)
    hidden = jax.nn.gelu(hidden.astype(jnp.bfloat16))
    return jnp.dot(hidden, down_weight, preferred_element_type=jnp.float32)


def kernel(
    owners, verts, group,
    feats, cols, weights, graph_gain, lag_mix, time_gain, graph_up_far, graph_down_far, time_up_far, time_down_far,
    out, *scratch,
):
    layers = lag_mix.shape[0]
    full = scratch[:layers]
    (
        raw, blocks, sent_graph, window, sent_time,
        graph_up, graph_down, time_up, time_down, own_sem, far_sem, raw_sem, first_send, first_recv, a_send, a_recv, z_send, z_recv, b_send, b_recv, v_send, v_recv,
    ) = scratch[layers:]
    snaps, tiles, tile, width = feats.shape
    picks = weights.shape[2]
    lags = lag_mix.shape[1]
    chunks = tiles // group
    rows = window.shape[3]
    parts = tile // rows
    pieces = chunks * parts
    held = group * snaps
    unused = min(held - (lags - 1), snaps - 1)
    pair = 2 if group % 2 == 0 else 1
    groups = owners // group

    me = lax.axis_index("snap")
    core = lax.axis_index("vert")
    slot = me % group
    plane = me // group
    base = me - slot
    first_tile = core * tiles

    def far_copy(i, l):
        far, near = (
            (graph_up_far, graph_up), (graph_down_far, graph_down), (time_up_far, time_up), (time_down_far, time_down)
        )[i]
        return pltpu.make_async_copy(far.at[l], near.at[l], far_sem.at[i, l])

    def raw_copy(r):
        return pltpu.make_async_copy(weights.at[:, r], raw.at[:, r], raw_sem.at[r])

    own_copy = pltpu.make_async_copy(feats, full[0].at[:, pl.ds(first_tile, tiles)], own_sem)
    own_copy.start()
    for i in range(2):
        far_copy(i, 0).start()
    for h in range(chunks):
        for d in range(group):
            raw_copy(((slot + d) % group) * chunks + h).start()
    for l in range(layers):
        for i in range(4):
            if l > 0 or i > 1:
                far_copy(i, l).start()

    barrier = pltpu.get_barrier_semaphore()
    for d in range(1, group):
        pl.semaphore_signal(barrier, inc=1, device_id=(base + (slot + d) % group, core), device_id_type=MESH)
    for q in range(1, verts):
        pl.semaphore_signal(barrier, inc=1, device_id=(me, (core + q) % verts), device_id_type=MESH)

    @pl.when(plane > 0)
    def _():
        pl.semaphore_signal(barrier, inc=1, device_id=(me - group, core), device_id_type=MESH)

    @pl.when(plane < groups - 1)
    def _():
        pl.semaphore_signal(barrier, inc=1, device_id=(me + group, core), device_id_type=MESH)

    ahead = jnp.where(plane < groups - 1, 1, 0)
    behind = jnp.where(plane > 0, 1, 0)
    pl.semaphore_wait(barrier, group - 1 + verts - 1 + ahead + behind)

    def first_copy(q):
        return pltpu.make_async_remote_copy(
            src_ref=feats,
            dst_ref=full[0].at[:, pl.ds(first_tile, tiles)],
            send_sem=first_send.at[q],
            recv_sem=first_recv.at[q],
            device_id=(me, (core + q) % verts),
            device_id_type=MESH,
        )

    for q in range(1, verts):
        first_copy(q).start()

    @pl.when(plane == 0)
    def _():
        for l in range(layers):
            for h in range(pieces):
                window[l, h, 0:held] = jnp.zeros((held, rows, width), jnp.bfloat16)

    own_copy.wait()
    for q in range(1, verts):
        first_copy(q).wait_recv()

    def a_copy(l, h, d):
        return pltpu.make_async_remote_copy(
            src_ref=sent_graph.at[l, h, d],
            dst_ref=window.at[l, h, pl.ds(held + slot * snaps, snaps)],
            send_sem=a_send.at[l, h, d],
            recv_sem=a_recv.at[l, h, d],
            device_id=(base + (slot + d) % group, core),
            device_id_type=MESH,
        )

    def z_part(l, h, d, origin, skip):
        return pltpu.make_async_remote_copy(
            src_ref=window.at[l, h, pl.ds(held + origin * snaps + skip, snaps - skip)],
            dst_ref=window.at[l, h, pl.ds(origin * snaps + skip, snaps - skip)],
            send_sem=z_send.at[l, h, d],
            recv_sem=z_recv.at[l, h, d],
            device_id=(jnp.minimum(me + group, owners - 1), core),
            device_id_type=MESH,
        )

    def z_do(l, h, d, act):
        origin = (slot + group - d) % group
        if unused == 0:
            act(z_part(l, h, d, origin, 0))
            return

        @pl.when(origin == 0)
        def _():
            act(z_part(l, h, d, 0, unused))

        @pl.when(origin > 0)
        def _():
            act(z_part(l, h, d, origin, 0))

    def spot(l, owner, h):
        target = out if l == layers - 1 else full[l + 1]
        first = 0 if l == layers - 1 else first_tile
        return target.at[:, first + owner * chunks + h // parts, pl.ds((h % parts) * rows, rows)]

    def b_copy(l, h, d):
        return pltpu.make_async_remote_copy(
            src_ref=sent_time.at[l, h, d],
            dst_ref=spot(l, slot, h),
            send_sem=b_send.at[l, h, d],
            recv_sem=b_recv.at[l, h, d],
            device_id=(base + (slot + d) % group, core),
            device_id_type=MESH,
        )

    def v_copy(l, h, d, q):
        piece = spot(l, (slot + group - d) % group, h)
        return pltpu.make_async_remote_copy(
            src_ref=piece,
            dst_ref=piece,
            send_sem=v_send.at[l, h, d, q],
            recv_sem=v_recv.at[l, h, d, q],
            device_id=(me, (core + q) % verts),
            device_id_type=MESH,
        )

    def hand_on(l, h, d):
        @pl.when(plane < groups - 1)
        def _():
            z_do(l, h, d, lambda copy: copy.start())

    def share(l, h, d):
        if l < layers - 1:
            for q in range(1, verts):
                v_copy(l, h, d, q).start()

    for l in range(layers):
        for i in range(2):
            far_copy(i, l).wait()

        def graph_step(h, d):
            r = ((slot + d) % group) * chunks + h
            if l == 0:
                raw_copy(r).wait()
            sums = []
            for t in range(snaps):
                if l == 0:
                    block = jnp.concatenate(
                        [raw[t, r, k].astype(jnp.float32).astype(jnp.bfloat16) for k in range(picks)], axis=1
                    )
                    blocks[t, r] = block
                else:
                    block = blocks[t, r]
                picked = jnp.concatenate([full[l][t, cols[t, r, k]] for k in range(picks)], axis=0)
                sums.append(jnp.dot(block, picked, preferred_element_type=jnp.float32))
            summed = jnp.concatenate(sums, axis=0)
            branch = mlp(normalise(summed, graph_gain[l:l + 1]), graph_up[l], graph_down[l])
            state = full[l][:, first_tile + r].astype(jnp.float32)
            result = (state + branch.reshape(snaps, tile, width)).astype(jnp.bfloat16)

            for p in range(parts):
                part = result[:, p * rows:(p + 1) * rows]
                if d == 0:
                    window[l, h * parts + p, pl.ds(held + slot * snaps, snaps)] = part
                    hand_on(l, h * parts + p, d)
                else:
                    sent_graph[l, h * parts + p, d] = part
                    a_copy(l, h * parts + p, d).start()

        order = [(h, d) for h in range(chunks) for d in range(1, group)]
        for h in range(chunks):
            order.insert(2 * h + 1, (h, 0))
        for h, d in order:
            graph_step(h, d)
            if h > 0 and d > 0:
                for p in range(parts):
                    a_copy(l, (h - 1) * parts + p, d).wait_recv()
                    hand_on(l, (h - 1) * parts + p, d)
        for p in range(parts):
            for d in range(1, group):
                a_copy(l, pieces - parts + p, d).wait_recv()
                hand_on(l, pieces - parts + p, d)
        for i in range(2, 4):
            far_copy(i, l).wait()

        def time_step(h, first):
            if first == 0:

                @pl.when(plane > 0)
                def _():
                    for e in range(group):
                        z_do(l, h, e, lambda copy: copy.wait_recv())

            mixes, states = [], []
            for c in range(pair):
                owner = (slot + first + c + 1) % group
                for t in range(snaps):
                    newest = held + owner * snaps + t
                    mixed = lag_mix[l, 0:1] * window[l, h, newest].astype(jnp.float32)
                    for m in range(1, lags):
                        mixed = mixed + lag_mix[l, m:m + 1] * window[l, h, newest - m].astype(jnp.float32)
                    mixes.append(mixed)
                    states.append(window[l, h, newest].astype(jnp.float32))
            branch = mlp(normalise(jnp.concatenate(mixes, axis=0), time_gain[l:l + 1]), time_up[l], time_down[l])
            result = (jnp.concatenate(states, axis=0) + branch).astype(jnp.bfloat16)
            result = result.reshape(pair, snaps, rows, width)

            for c in range(pair):
                d = (first + c + 1) % group

                def keep(c=c, d=d):
                    spot(l, slot, h)[...] = result[c]
                    share(l, h, d)

                def send(c=c, d=d):
                    sent_time[l, h, d] = result[c]
                    b_copy(l, h, d).start()

                keep() if d == 0 else send()

        for h in range(pieces):
            for first in range(0, group, pair):
                time_step(h, first)
        for h in range(pieces):
            for d in range(1, group):
                b_copy(l, h, d).wait_recv()
                share(l, h, d)
        if l < layers - 1:
            for h in range(pieces):
                for d in range(group):
                    for q in range(1, verts):
                        v_copy(l, h, d, q).wait_recv()

    for q in range(1, verts):
        first_copy(q).wait_send()
    for l in range(layers):
        for h in range(pieces):
            for d in range(1, group):
                a_copy(l, h, d).wait_send()
                b_copy(l, h, d).wait_send()
            for d in range(group):
                if l < layers - 1:
                    for q in range(1, verts):
                        v_copy(l, h, d, q).wait_send()

                @pl.when(plane < groups - 1)
                def _():
                    z_do(l, h, d, lambda copy: copy.wait_send())


def on_device(owners, verts, features, tile_cols, tile_weights, graph_gain, graph_up, graph_down, lag_mix, time_gain, time_up, time_down):
    snaps, vert_dev, width = features.shape
    _, tiles, picks, tile, _ = tile_weights.shape
    layers, lags = lag_mix.shape[0], lag_mix.shape[1]
    group = -(-(lags - 1) // snaps)
    while owners % group or tiles % group:
        group += 1
    rows = tile
    pieces = tiles // group
    held = group * snaps
    vmem = pl.BlockSpec(memory_space=pltpu.VMEM)
    far = pl.BlockSpec(memory_space=pl.ANY)
    bf16 = jnp.bfloat16
    dma = pltpu.SemaphoreType.DMA
    result = pl.pallas_call(
        functools.partial(kernel, owners, verts, group),
        out_shape=jax.ShapeDtypeStruct((snaps, tiles, tile, width), bf16),
        in_specs=[far, pl.BlockSpec(memory_space=pltpu.SMEM), far, vmem, vmem, vmem] + [far] * 4,
        out_specs=vmem,
        scratch_shapes=[pltpu.VMEM((snaps, verts * tiles, tile, width), bf16)] * layers + [
            pltpu.VMEM((snaps, tiles, picks, tile, tile), jnp.int32),
            pltpu.VMEM((snaps, tiles, tile, picks * tile), bf16),
            pltpu.VMEM((layers, pieces, group, snaps, rows, width), bf16),
            pltpu.VMEM((layers, pieces, 2 * held, rows, width), bf16),
            pltpu.VMEM((layers, pieces, group, snaps, rows, width), bf16),
            pltpu.VMEM(graph_up.shape, bf16),
            pltpu.VMEM(graph_down.shape, bf16),
            pltpu.VMEM(time_up.shape, bf16),
            pltpu.VMEM(time_down.shape, bf16),
            dma,
            dma((4, layers)),
            dma((tiles,)),
            dma((verts,)),
            dma((verts,)),
        ] + [dma((layers, pieces, group))] * 6 + [dma((layers, pieces, group, verts))] * 2,
        compiler_params=pltpu.CompilerParams(
            collective_id=0, has_side_effects=True, vmem_limit_bytes=60 * 1024 * 1024
        ),
    )(
        features.reshape(snaps, tiles, tile, width), tile_cols, tile_weights,
        graph_gain, lag_mix, time_gain, graph_up, graph_down, time_up, time_down,
    )
    return result.reshape(features.shape)


def solution(mesh):
    return jax.shard_map(
        functools.partial(on_device, mesh.shape["snap"], mesh.shape["vert"]),
        mesh=mesh,
        in_specs=(
            P("snap", "vert", None),
            P("snap", "vert", None),
            P("snap", "vert", None, None, None),
        ) + (P(),) * 7,
        out_specs=P("snap", "vert", None),
        check_vma=False,
    )
```

profile of v0, /device:TPU:16, one launch (start us, length us, event | category | flops | bytes accessed | tf_op | source)
XLA Modules:
  0.0 48.9 jit_solution(5584637647629329391)
XLA Ops:
  0.0 47.0 %shard_map.100 = bf16[2,8,128,128]{3,2,1,0:T(8,128)(2,1)} custom-call(bf16[2,8,128,128]{3,2,1,0:T(8,128)(2,1)} %bitcast.3, s32[2,8,8]{2,1,0:T(8,128)} %cols.1, s32[2,8,8,128,128]{4,3,2,1,0:T(8,128)} %weights.1, f32[2,128]{1,0:T(2,128)} %graph_gain.1, f32[2,8,128]{2,1,0:T(8,128)} %lag_mix.1, f32[2,128]{1,0:T(2,128)} %time_gain.1, ...), custom_call_target="tpu_custom_call" | custom-call | tf_op jit(solution)/shard_map/pallas_call | solution.py:315
  47.0 1.9 %copy.12 = bf16[2,1024,128]{2,1,0:T(8,128)(2,1)} copy(bf16[2,1024,128]{2,1,0:T(8,128)(2,1)} %bitcast.2) | data formatting | bytes 1048576
where the time goes:
time: 49.8 us; the launch traced here: 48.9 us
  Pallas kernels  47 us (94%)
  local copies, waits for them, and re-layouts  1.87 us (4%)
    pallas_call x1, Pallas kernels, on_device(): pl.pallas_call(functools.partial(kernel, owners, verts, group), out_shape...  47 us
    unnamed x1, local copies, waits for them, and re-layouts  1.87 us

commit v1 on v0

v1 whole, which is shorter than its diff:
```python
import functools

import jax
import jax.numpy as jnp
from jax import lax
from jax.experimental import pallas as pl
from jax.experimental.pallas import tpu as pltpu
from jax.sharding import PartitionSpec as P

eps = 1e-06
MESH = pl.DeviceIdType.MESH
STRIP = 16


def normalise(rows, gain_row):
    scale = lax.rsqrt(jnp.mean(rows * rows, axis=-1, keepdims=True) + eps)
    return (rows * scale * gain_row).astype(jnp.bfloat16)


def mlp(normed, up_weight, down_weight):
    hidden = jnp.dot(normed, up_weight, preferred_element_type=jnp.float32)
    hidden = jax.nn.gelu(hidden.astype(jnp.bfloat16))
    return jnp.dot(hidden, down_weight, preferred_element_type=jnp.float32)


def kernel(
    owners, verts, group,
    feats, cols_far, weights, graph_gain_far, lag_mix_far, time_gain_far, graph_up_far, graph_down_far, time_up_far, time_down_far,
    out, *scratch,
):
    layers = lag_mix_far.shape[0]
    full = scratch[:layers]
    (
        raw, blocks, sent_graph, window, sent_time,
        graph_up, graph_down, time_up, time_down, own_sem, far_sem, raw_sem, first_send, first_recv,
        a_send, a_recv, z_send, z_recv, b_send, b_recv, v_send, v_recv, out_sem,
        cols, graph_gain, lag_mix, time_gain, small_sem,
    ) = scratch[layers:]
    snaps, tiles, tile, width = feats.shape
    picks = weights.shape[2]
    lags = lag_mix_far.shape[1]
    rows = window.shape[3]
    held = group * snaps
    unused = held - (lags - 1)
    groups = owners // group
    ahead_tiles = tiles
    delay = min(5, tiles - 1)

    me = lax.axis_index("snap")
    core = lax.axis_index("vert")
    slot = me % group
    plane = me // group
    base = me - slot
    first_tile = core * tiles

    def strip(owner):
        return pl.ds(pl.multiple_of(owner * rows, rows), rows)

    def far_copy(i, l):
        far, near = (
            (graph_up_far, graph_up), (graph_down_far, graph_down), (time_up_far, time_up), (time_down_far, time_down)
        )[i]
        return pltpu.make_async_copy(far.at[l], near.at[l], far_sem.at[i, l])

    def raw_copy(r):
        return pltpu.make_async_copy(weights.at[:, r], raw.at[:, r], raw_sem.at[r])

    smalls = [
        pltpu.make_async_copy(src, dst, small_sem.at[i])
        for i, (src, dst) in enumerate(
            [(cols_far, cols), (graph_gain_far, graph_gain), (lag_mix_far, lag_mix), (time_gain_far, time_gain)]
        )
    ]
    own_copy = pltpu.make_async_copy(feats, full[0].at[:, pl.ds(first_tile, tiles)], own_sem)
    barrier = pltpu.get_barrier_semaphore()
    for q in range(1, verts):
        pl.semaphore_signal(barrier, inc=1, device_id=(me, (core + q) % verts), device_id_type=MESH)
    for d in range(1, group):
        pl.semaphore_signal(barrier, inc=1, device_id=(base + (slot + d) % group, core), device_id_type=MESH)

    @pl.when(plane > 0)
    def _():
        pl.semaphore_signal(barrier, inc=1, device_id=(me - group, core), device_id_type=MESH)

    @pl.when(plane < groups - 1)
    def _():
        pl.semaphore_signal(barrier, inc=1, device_id=(me + group, core), device_id_type=MESH)

    own_copy.start()
    for copy in smalls:
        copy.start()
    raw_copy(0).start()
    for i in range(2):
        far_copy(i, 0).start()
    for r in range(1, tiles):
        raw_copy(r).start()
    for l in range(layers):
        for i in range(4):
            if l > 0 or i > 1:
                far_copy(i, l).start()

    @pl.when(plane == 0)
    def _():
        for l in range(layers):
            for r in range(tiles):
                window[l, r, 0:held] = jnp.zeros((held, rows, width), jnp.bfloat16)

    ahead = jnp.where(plane < groups - 1, 1, 0)
    behind = jnp.where(plane > 0, 1, 0)
    with jax.named_scope("barrier"):
        pl.semaphore_wait(barrier, group - 1 + verts - 1 + ahead + behind)

    def first_copy(q):
        return pltpu.make_async_remote_copy(
            src_ref=feats,
            dst_ref=full[0].at[:, pl.ds(first_tile, tiles)],
            send_sem=first_send.at[q],
            recv_sem=first_recv.at[q],
            device_id=(me, (core + q) % verts),
            device_id_type=MESH,
        )

    for q in range(1, verts):
        first_copy(q).start()

    def convert(r):
        raw_copy(r).wait()
        for t in range(snaps):
            blocks[t, r] = jnp.concatenate(
                [raw[t, r, k].astype(jnp.float32).astype(jnp.bfloat16) for k in range(picks)], axis=1
            )

    early = min(3, tiles)
    for r in range(early):
        with jax.named_scope(f"k{r}"):
            convert(r)

    with jax.named_scope("first"):
        for copy in smalls:
            copy.wait()
        own_copy.wait()
        for q in range(1, verts):
            first_copy(q).wait_recv()

    def a_copy(l, r, d):
        owner = (slot + d) % group
        return pltpu.make_async_remote_copy(
            src_ref=sent_graph.at[l, r, :, strip(owner)],
            dst_ref=window.at[l, r, pl.ds(held + slot * snaps, snaps)],
            send_sem=a_send.at[l, r],
            recv_sem=a_recv.at[l, r],
            device_id=(base + owner, core),
            device_id_type=MESH,
        )

    def a_all(l, r):
        part = window.at[l, r, pl.ds(0, (group - 1) * snaps)]
        return pltpu.make_async_remote_copy(
            src_ref=part, dst_ref=part, send_sem=a_send.at[l, r], recv_sem=a_recv.at[l, r],
            device_id=(base + (slot + 1) % group, core), device_id_type=MESH,
        )

    def z_copy(l, r, start, count):
        return pltpu.make_async_remote_copy(
            src_ref=window.at[l, r, pl.ds(held + start, count)],
            dst_ref=window.at[l, r, pl.ds(start, count)],
            send_sem=z_send.at[l, r],
            recv_sem=z_recv.at[l, r],
            device_id=(jnp.minimum(me + group, owners - 1), core),
            device_id_type=MESH,
        )

    def z_all(l, r):
        return z_copy(l, r, unused, held - unused)

    def z_origin(l, r, origin):
        if unused == 0:
            z_copy(l, r, origin * snaps, snaps).start()
            return

        @pl.when(origin == 0)
        def _():
            z_copy(l, r, unused, snaps - unused).start()

        @pl.when(origin > 0)
        def _():
            z_copy(l, r, origin * snaps, snaps).start()

    def b_copy(l, r, d):
        home = (slot + d) % group
        target = out.at[:, r] if l == layers - 1 else full[l + 1].at[:, first_tile + r]
        return pltpu.make_async_remote_copy(
            src_ref=sent_time.at[l, r, pl.ds(home * snaps, snaps)],
            dst_ref=target.at[:, strip(slot)],
            send_sem=b_send.at[l, r],
            recv_sem=b_recv.at[l, r],
            device_id=(base + home, core),
            device_id_type=MESH,
        )

    def out_copy(r):
        own = sent_time.at[layers - 1, r, pl.ds(slot * snaps, snaps)]
        return pltpu.make_async_copy(own, out.at[:, r, strip(slot)], out_sem.at[r])

    def b_all(l, r):
        part = sent_time.at[l, r, pl.ds(0, (group - 1) * snaps)]
        return pltpu.make_async_remote_copy(
            src_ref=part, dst_ref=part, send_sem=b_send.at[l, r], recv_sem=b_recv.at[l, r],
            device_id=(base + (slot + 1) % group, core), device_id_type=MESH,
        )

    def v_copy(l, r, q):
        piece = full[l + 1].at[:, first_tile + r]
        return pltpu.make_async_remote_copy(
            src_ref=piece,
            dst_ref=piece,
            send_sem=v_send.at[l, r, q],
            recv_sem=v_recv.at[l, r, q],
            device_id=(me, (core + q) % verts),
            device_id_type=MESH,
        )

    def graph_step(l, r):
        if l == 0 and r >= early:
            convert(r)
        sums = []
        for t in range(snaps):
            picked = jnp.concatenate([full[l][t, cols[t, r, k]] for k in range(picks)], axis=0)
            sums.append(jnp.dot(blocks[t, r], picked, preferred_element_type=jnp.float32))
        summed = jnp.concatenate(sums, axis=0)
        branch = mlp(normalise(summed, graph_gain[l:l + 1]), graph_up[l], graph_down[l])
        state = full[l][:, first_tile + r].astype(jnp.float32)
        sent_graph[l, r] = (state + branch.reshape(snaps, tile, width)).astype(jnp.bfloat16)
        for d in range(1, group):
            a_copy(l, r, d).start()
        window[l, r, pl.ds(held + slot * snaps, snaps)] = sent_graph[l, r, :, strip(slot)]
        if r < ahead_tiles:

            @pl.when(plane < groups - 1)
            def _():
                z_origin(l, r, slot)

    def forward(l, r):
        a_all(l, r).wait_recv()

        @pl.when(plane < groups - 1)
        def _():
            if r < ahead_tiles:
                for d in range(1, group):
                    z_origin(l, r, (slot + d) % group)
            else:
                z_all(l, r).start()

    def time_step(l, batch):
        for r in batch:

            @pl.when(plane > 0)
            def _():
                z_all(l, r).wait_recv()

        spots, mixes, states = [], [], []
        for r in batch:
            for top in range(0, rows, STRIP):
                span = slice(top, top + STRIP)
                seen = {i: window[l, r, i, span].astype(jnp.float32) for i in range(unused, 2 * held)}
                for i in range(held):
                    mixed = lag_mix[l, 0:1] * seen[held + i]
                    for m in range(1, lags):
                        mixed = mixed + lag_mix[l, m:m + 1] * seen[held + i - m]
                    spots.append((r, i, span))
                    mixes.append(mixed)
                    states.append(seen[held + i])
        branch = mlp(normalise(jnp.concatenate(mixes, axis=0), time_gain[l:l + 1]), time_up[l], time_down[l])
        result = (jnp.concatenate(states, axis=0) + branch).astype(jnp.bfloat16)
        for n, (r, i, span) in enumerate(spots):
            sent_time[l, r, i, span] = result[n * STRIP:(n + 1) * STRIP]
        for r in batch:
            for d in range(1, group):
                b_copy(l, r, d).start()
            if l == layers - 1:
                out_copy(r).start()
            else:
                own = sent_time[l, r, pl.ds(slot * snaps, snaps)]
                full[l + 1][:, first_tile + r, strip(slot)] = own

    def collect(l, r):
        b_all(l, r).wait_recv()
        if l < layers - 1:
            for q in range(1, verts):
                v_copy(l, r, q).start()

    for l in range(layers):
        for i in range(2):
            far_copy(i, l).wait()
        for r in range(tiles):
            with jax.named_scope(f"g{l}_{r}"):
                graph_step(l, r)
            if r >= delay:
                with jax.named_scope(f"f{l}_{r - delay}"):
                    forward(l, r - delay)
        for i in range(2, 4):
            far_copy(i, l).wait()
        passed = tiles - delay
        for r in range(tiles):
            while passed < tiles and passed <= delay + r:
                with jax.named_scope(f"f{l}_{passed}"):
                    forward(l, passed)
                passed += 1
            with jax.named_scope(f"t{l}_{r}"):
                time_step(l, [r])
        for r in range(tiles):
            with jax.named_scope(f"c{l}_{r}"):
                collect(l, r)
        if l < layers - 1:
            with jax.named_scope(f"v{l}"):
                for r in range(tiles):
                    for q in range(1, verts):
                        v_copy(l, r, q).wait_recv()

    with jax.named_scope("drain"):
        for q in range(1, verts):
            first_copy(q).wait_send()
        for r in range(tiles):
            out_copy(r).wait()
        for l in range(layers):
            for r in range(tiles):
                a_all(l, r).wait_send()
                b_all(l, r).wait_send()
                if l < layers - 1:
                    for q in range(1, verts):
                        v_copy(l, r, q).wait_send()

                @pl.when(plane < groups - 1)
                def _():
                    z_all(l, r).wait_send()


def on_device(owners, verts, features, tile_cols, tile_weights, graph_gain, graph_up, graph_down, lag_mix, time_gain, time_up, time_down):
    snaps, vert_dev, width = features.shape
    _, tiles, picks, tile, _ = tile_weights.shape
    layers, lags = lag_mix.shape[0], lag_mix.shape[1]
    group = -(-(lags - 1) // snaps)
    while owners % group or tile % (group * STRIP):
        group += 1
    rows = tile // group
    held = group * snaps
    bf16 = jnp.bfloat16
    dma = pltpu.SemaphoreType.DMA
    result = pl.pallas_call(
        functools.partial(kernel, owners, verts, group),
        out_shape=jax.ShapeDtypeStruct((snaps, tiles, tile, width), bf16),
        in_specs=[pl.BlockSpec(memory_space=pltpu.HBM)] * 10,
        out_specs=pl.BlockSpec(memory_space=pl.ANY),
        scratch_shapes=[pltpu.VMEM((snaps, verts * tiles, tile, width), bf16)] * layers + [
            pltpu.VMEM((snaps, tiles, picks, tile, tile), jnp.int32),
            pltpu.VMEM((snaps, tiles, tile, picks * tile), bf16),
            pltpu.VMEM((layers, tiles, snaps, tile, width), bf16),
            pltpu.VMEM((layers, tiles, 2 * held, rows, width), bf16),
            pltpu.VMEM((layers, tiles, held, rows, width), bf16),
            pltpu.VMEM(graph_up.shape, bf16),
            pltpu.VMEM(graph_down.shape, bf16),
            pltpu.VMEM(time_up.shape, bf16),
            pltpu.VMEM(time_down.shape, bf16),
            dma,
            dma((4, layers)),
            dma((tiles,)),
            dma((verts,)),
            dma((verts,)),
        ] + [dma((layers, tiles))] * 6 + [dma((layers, tiles, verts))] * 2 + [dma((tiles,))] + [
            pltpu.SMEM(tile_cols.shape, jnp.int32),
            pltpu.VMEM(graph_gain.shape, jnp.float32),
            pltpu.VMEM(lag_mix.shape, jnp.float32),
            pltpu.VMEM(time_gain.shape, jnp.float32),
            dma((4,)),
        ],
        compiler_params=pltpu.CompilerParams(
            collective_id=0, has_side_effects=True, vmem_limit_bytes=36 * 1024 * 1024
        ),
    )(
        *[pltpu.with_memory_space_constraint(array, pltpu.HBM) for array in (
            features.reshape(snaps, tiles, tile, width), tile_cols, tile_weights,
            graph_gain, lag_mix, time_gain, graph_up, graph_down, time_up, time_down,
        )]
    )
    return result.reshape(features.shape)


def solution(mesh):
    return jax.shard_map(
        functools.partial(on_device, mesh.shape["snap"], mesh.shape["vert"]),
        mesh=mesh,
        in_specs=(
            P("snap", "vert", None),
            P("snap", "vert", None),
            P("snap", "vert", None, None, None),
        ) + (P(),) * 7,
        out_specs=P("snap", "vert", None),
        check_vma=False,
    )
```

time: 49.8 us -> 43.3 us (0.87); the launches traced: 48.9 us -> 42.9 us
  Pallas kernels: 47 us -> 42.1 us
  local copies, waits for them, and re-layouts: 1.87 us -> 0.8 us
    pallas_call x1, Pallas kernels: 47 us -> 42.1 us  [on_device(): pl.pallas_call(functools.partial(kernel, owners, verts, group), out_shape...]
    unnamed x1, local copies, waits for them, and re-layouts: 1.87 us -> 0.8 us
where the time goes in v1:
time: 43.3 us; the launch traced here: 42.9 us
  Pallas kernels  42.1 us (97%)
  local copies, waits for them, and re-layouts  0.8 us (2%)
    pallas_call x1, Pallas kernels, on_device(): pl.pallas_call(functools.partial(kernel, owners, verts, group), out_shape...  42.1 us

profile of v1, /device:TPU:16, one launch (start us, length us, event | category | flops | bytes accessed | tf_op | source)
XLA Modules:
  0.0 42.9 jit_solution(6028800522670913589)
XLA Ops:
  0.0 42.1 %shard_map.100 = bf16[2,8,128,128]{3,2,1,0:T(8,128)(2,1)S(1)} custom-call(bf16[2,8,128,128]{3,2,1,0:T(8,128)(2,1)} %bitcast.3, s32[2,8,8]{2,1,0:T(8,128)} %cols_far.1, s32[2,8,8,128,128]{4,3,2,1,0:T(8,128)} %weights.1, f32[2,128]{1,0:T(2,128)} %graph_gain_far.1, f32[2,8,128]{2,1,0:T(8,128)} %lag_mix_far.1, f32[2,128]{1,0:T(2,128)} %time_gain_far.1, ...), custom_call_target="tpu_custom_call" | custom-call | tf_op jit(solution)/shard_map/pallas_call | solution.py:349
  42.1 0.8 %copy.12 = bf16[2,1024,128]{2,1,0:T(8,128)(2,1)} copy(bf16[2,1024,128]{2,1,0:T(8,128)(2,1)S(1)} %bitcast.2) | data formatting | bytes 1048576

commit v2 on v1

v2 whole, which is shorter than its diff:
```python
import functools

import jax
import jax.numpy as jnp
from jax import lax
from jax.experimental import pallas as pl
from jax.experimental.pallas import tpu as pltpu
from jax.sharding import PartitionSpec as P

eps = 1e-06
MESH = pl.DeviceIdType.MESH
STRIP = 16
EARLY = 3
BEHIND = 4


def normalise(rows, gain_row):
    scale = lax.rsqrt(jnp.mean(rows * rows, axis=-1, keepdims=True) + eps)
    return (rows * scale * gain_row).astype(jnp.bfloat16)


def mlp(normed, up_weight, down_weight):
    hidden = jnp.dot(normed, up_weight, preferred_element_type=jnp.float32)
    hidden = jax.nn.gelu(hidden.astype(jnp.bfloat16))
    return jnp.dot(hidden, down_weight, preferred_element_type=jnp.float32)


def kernel(
    owners, verts, group,
    feats, cols_far, weights, graph_gain_far, lag_mix_far, time_gain_far, graph_up_far, graph_down_far, time_up_far, time_down_far,
    out, *scratch,
):
    layers = lag_mix_far.shape[0]
    full = scratch[:layers]
    (
        raw, blocks, sent_graph, window, sent_time,
        graph_up, graph_down, time_up, time_down, own_sem, far_sem, raw_sem, first_send, first_recv,
        a_send, a_recv, a_soon, cross_send, cross_recv, z_send, z_recv, b_send, b_recv, v_send, v_recv, out_sem,
        cols, graph_gain, lag_mix, time_gain, small_sem,
    ) = scratch[layers:]
    snaps, tiles, tile, width = feats.shape
    picks = weights.shape[2]
    lags = lag_mix_far.shape[1]
    rows = window.shape[3]
    held = group * snaps
    unused = held - (lags - 1)
    groups = owners // group
    early = min(EARLY, tiles)
    skip = min(unused, snaps - 1)

    me = lax.axis_index("snap")
    core = lax.axis_index("vert")
    slot = me % group
    plane = me // group
    base = me - slot
    first_tile = core * tiles

    def partner(d, back=False):
        if group == 4:
            return (slot + d) % 2 + 2 * ((slot // 2 + d // 2) % 2)
        return (slot + (group - d if back else d)) % group

    def strip(owner):
        return pl.ds(pl.multiple_of(owner * rows, rows), rows)

    def far_copy(i, l):
        far, near = (
            (graph_up_far, graph_up), (graph_down_far, graph_down), (time_up_far, time_up), (time_down_far, time_down)
        )[i]
        return pltpu.make_async_copy(far.at[l], near.at[l], far_sem.at[i, l])

    def raw_copy(r):
        return pltpu.make_async_copy(weights.at[:, r], raw.at[:, r], raw_sem.at[r])

    smalls = [
        pltpu.make_async_copy(src, dst, small_sem.at[i])
        for i, (src, dst) in enumerate(
            [(cols_far, cols), (graph_gain_far, graph_gain), (lag_mix_far, lag_mix), (time_gain_far, time_gain)]
        )
    ]
    own_copy = pltpu.make_async_copy(feats, full[0].at[:, pl.ds(first_tile, tiles)], own_sem)
    barrier = pltpu.get_barrier_semaphore()
    for q in range(verts):
        for d in range(group):
            if q + d > 0:
                pl.semaphore_signal(
                    barrier, inc=1, device_id=(base + partner(d), (core + q) % verts), device_id_type=MESH
                )

    @pl.when(plane > 0)
    def _():
        pl.semaphore_signal(barrier, inc=1, device_id=(me - group, core), device_id_type=MESH)

    @pl.when(plane < groups - 1)
    def _():
        pl.semaphore_signal(barrier, inc=1, device_id=(me + group, core), device_id_type=MESH)

    own_copy.start()
    for copy in smalls:
        copy.start()
    soon = min(2, tiles)
    for r in range(soon):
        raw_copy(r).start()
    for i in range(2):
        far_copy(i, 0).start()

    @pl.when(plane == 0)
    def _():
        for l in range(layers):
            for w in range(tiles):
                window[l, w, 0:held] = jnp.zeros((held, rows, width), jnp.bfloat16)

    ahead = jnp.where(plane < groups - 1, 1, 0)
    behind = jnp.where(plane > 0, 1, 0)
    with jax.named_scope("barrier"):
        pl.semaphore_wait(barrier, group * verts - 1 + ahead + behind)

    def first_copy(q):
        return pltpu.make_async_remote_copy(
            src_ref=feats,
            dst_ref=full[0].at[:, pl.ds(first_tile, tiles)],
            send_sem=first_send.at[q - 1],
            recv_sem=first_recv.at[q - 1],
            device_id=(me, (core + q) % verts),
            device_id_type=MESH,
        )

    for q in range(1, verts):
        first_copy(q).start()
    for r in range(soon, tiles):
        raw_copy(r).start()
    for l in range(layers):
        for i in range(4):
            if l > 0 or i > 1:
                far_copy(i, l).start()

    def convert(r):
        raw_copy(r).wait()
        for t in range(snaps):
            blocks[t, r] = jnp.concatenate(
                [raw[t, r, k].astype(jnp.float32).astype(jnp.bfloat16) for k in range(picks)], axis=1
            )

    with jax.named_scope("k0"):
        convert(0)

    with jax.named_scope("first"):
        for copy in smalls:
            copy.wait()
        own_copy.wait()
        for q in range(1, verts):
            first_copy(q).wait_recv()

    def remote(src, dst, send_sem, recv_sem, device):
        return pltpu.make_async_remote_copy(
            src_ref=src, dst_ref=dst, send_sem=send_sem, recv_sem=recv_sem, device_id=device, device_id_type=MESH
        )

    beside = (base + (slot + 1) % group, core)
    onward = (jnp.minimum(me + group, owners - 1), core)
    others = (group - 1) * snaps

    def a_copy(l, w, d):
        owner = partner(d)
        arrived = a_soon.at[l, w, d - 1] if w < early else a_recv.at[l, w]
        return remote(
            sent_graph.at[l, w, :, strip(owner)], window.at[l, w, pl.ds(held + slot * snaps, snaps)],
            a_send, arrived, (base + owner, core),
        )

    def a_all(l, w):
        part = window.at[l, w, pl.ds(0, others)]
        return remote(part, part, a_send, a_recv.at[l, w], beside)

    def z_copy(l, w, start, count):
        return remote(
            window.at[l, w, pl.ds(held + start, count)], window.at[l, w, pl.ds(start, count)],
            z_send, z_recv.at[l, w], onward,
        )

    def z_all(l, w):
        return z_copy(l, w, unused, held - unused)

    def z_origin(l, w, origin):
        if unused == 0:
            z_copy(l, w, origin * snaps, snaps).start()
            return

        @pl.when(origin == 0)
        def _():
            z_copy(l, w, skip, snaps - skip).start()

        @pl.when(origin > 0)
        def _():
            z_copy(l, w, origin * snaps, snaps).start()

    def b_mark(l, w):
        return l * tiles + w if l < layers - 1 else (layers - 1) * tiles

    def target(l, w):
        place = out.at[:, w] if l == layers - 1 else full[l + 1].at[:, first_tile + w]
        return place.at[:, strip(slot)]

    def b_copy(l, w, d):
        home = partner(d)
        return remote(
            sent_time.at[l, w, pl.ds(home * snaps, snaps)], target(l, w),
            b_send, b_recv.at[b_mark(l, w)], (base + home, core),
        )

    def cross_copy(l, d, q):
        home = partner(d)
        return remote(
            sent_time.at[l, tiles - 1, pl.ds(home * snaps, snaps)], target(l, tiles - 1),
            cross_send.at[l, q - 1], cross_recv.at[l, q - 1], (base + home, (core + q) % verts),
        )

    def cross_all(l, q):
        part = full[l + 1].at[:, first_tile + tiles - 1]
        return remote(part, part, cross_send.at[l, q - 1], cross_recv.at[l, q - 1], (me, (core + q) % verts))

    def b_all(l, w):
        part = sent_time.at[l, w, pl.ds(0, others)] if l < layers - 1 else sent_time.at[l, :, pl.ds(0, others)]
        return remote(part, part, b_send, b_recv.at[b_mark(l, w)], beside)

    def out_copy(w):
        own = sent_time.at[layers - 1, w, pl.ds(slot * snaps, snaps)]
        return pltpu.make_async_copy(own, out.at[:, w, strip(slot)], out_sem)

    def v_copy(l, part, q):
        return remote(part, part, v_send.at[l, q - 1], v_recv.at[l, q - 1], (me, (core + q) % verts))

    def v_all(l, q):
        return v_copy(l, full[l + 1].at[:, pl.ds(first_tile, tiles - 1)], q)

    def v_start(l, r):
        for q in range(1, verts):
            v_copy(l, full[l + 1].at[:, first_tile + r], q).start()

    def graph_step(l, r):
        if l == 0 and r > 0:
            convert(r)
        sums = []
        for t in range(snaps):
            picked = jnp.concatenate([full[l][t, cols[t, r, k]] for k in range(picks)], axis=0)
            sums.append(jnp.dot(blocks[t, r], picked, preferred_element_type=jnp.float32))
        summed = jnp.concatenate(sums, axis=0)
        branch = mlp(normalise(summed, graph_gain[l:l + 1]), graph_up[l], graph_down[l])
        state = full[l][:, first_tile + r].astype(jnp.float32)
        result = (state + branch.reshape(snaps, tile, width)).astype(jnp.bfloat16)
        sent_graph[l, r] = result
        for d in range(1, group):
            a_copy(l, r, d).start()
        window[l, r, pl.ds(held + slot * snaps, snaps)] = sent_graph[l, r, :, strip(slot)]

        @pl.when(plane < groups - 1)
        def _():
            z_origin(l, r, slot)

    def forward(l, w, parts):
        if w >= early:
            a_all(l, w).wait_recv()
        else:
            for d in parts:
                a_copy(l, w, d).wait_recv()

        @pl.when(plane < groups - 1)
        def _():
            for d in parts:
                z_origin(l, w, partner(d, True))

    def forward_most(l, w):
        forward(l, w, range(1, group - 1))

    def forward_last(l, w):
        forward(l, w, [group - 1])

    def forward_all(l, w):
        forward(l, w, range(1, group))

    def time_step(l, w):
        @pl.when(plane > 0)
        def _():
            z_all(l, w).wait_recv()

        spots, mixes, states = [], [], []
        for top in range(0, rows, STRIP):
            span = slice(top, top + STRIP)
            seen = {i: window[l, w, i, span].astype(jnp.float32) for i in range(unused, 2 * held)}
            for i in range(held):
                mixed = lag_mix[l, 0:1] * seen[held + i]
                for m in range(1, lags):
                    mixed = mixed + lag_mix[l, m:m + 1] * seen[held + i - m]
                spots.append((i, span))
                mixes.append(mixed)
                states.append(seen[held + i])
        branch = mlp(normalise(jnp.concatenate(mixes, axis=0), time_gain[l:l + 1]), time_up[l], time_down[l])
        result = (jnp.concatenate(states, axis=0) + branch).astype(jnp.bfloat16)
        for n, (i, span) in enumerate(spots):
            sent_time[l, w, i, span] = result[n * STRIP:(n + 1) * STRIP]
        for d in range(1, group):
            b_copy(l, w, d).start()
        if l < layers - 1 and w == tiles - 1:
            for q in range(1, verts):
                for d in range(group):
                    cross_copy(l, d, q).start()
        if l == layers - 1:
            out_copy(w).start()
        else:
            own = sent_time[l, w, pl.ds(slot * snaps, snaps)]
            full[l + 1][:, first_tile + w, strip(slot)] = own

    def collect(l, w):
        b_all(l, w).wait_recv()
        if w < tiles - 1:
            v_start(l, w)

    def run(kind, step, l, n):
        with jax.named_scope(f"{kind}{l}_{n}"):
            step(l, n)

    for l in range(layers):
        for i in range(2):
            far_copy(i, l).wait()
        for r in range(tiles):
            run("g", graph_step, l, r)
            w = r - BEHIND
            if 1 <= w <= early:
                run("fl", forward_last, l, w - 1)
            if 0 <= w < early:
                run("fm", forward_most, l, w)
        for i in range(2, 4):
            far_copy(i, l).wait()
        for w in range(max(tiles - BEHIND, 0), early):
            run("fm", forward_most, l, w)
        for w in range(max(tiles - BEHIND - 1, 0), early):
            run("fl", forward_last, l, w)
        passed = early
        for w in range(tiles):
            while passed < min(w + BEHIND, tiles):
                run("f", forward_all, l, passed)
                passed += 1
            run("t", time_step, l, w)
        if l < layers - 1:
            for w in range(tiles):
                run("c", collect, l, w)
            with jax.named_scope(f"v{l}"):
                for q in range(1, verts):
                    cross_all(l, q).wait_recv()
                    v_all(l, q).wait_recv()
        else:
            with jax.named_scope(f"c{l}"):
                b_all(l, 0).wait_recv()

    with jax.named_scope("drain"):
        for q in range(1, verts):
            first_copy(q).wait_send()
        part = out.at[:, :, pl.ds(0, rows)]
        pltpu.make_async_copy(part, part, out_sem).wait()
        part = window.at[:, :, pl.ds(0, others)]
        remote(part, part, a_send, a_recv.at[0, 0], beside).wait_send()
        part = sent_time.at[:, :, pl.ds(0, others)]
        remote(part, part, b_send, b_recv.at[0], beside).wait_send()
        for l in range(layers - 1):
            for q in range(1, verts):
                v_all(l, q).wait_send()
                cross_all(l, q).wait_send()

        @pl.when(plane < groups - 1)
        def _():
            part = window.at[:, :, pl.ds(unused, held - unused)]
            remote(part, part, z_send, z_recv.at[0, 0], onward).wait_send()


def on_device(owners, verts, features, tile_cols, tile_weights, graph_gain, graph_up, graph_down, lag_mix, time_gain, time_up, time_down):
    snaps, vert_dev, width = features.shape
    _, tiles, picks, tile, _ = tile_weights.shape
    layers, lags = lag_mix.shape[0], lag_mix.shape[1]
    group = -(-(lags - 1) // snaps)
    while owners % group or tile % (group * STRIP):
        group += 1
    rows = tile // group
    held = group * snaps
    bf16 = jnp.bfloat16
    dma = pltpu.SemaphoreType.DMA
    result = pl.pallas_call(
        functools.partial(kernel, owners, verts, group),
        out_shape=jax.ShapeDtypeStruct((snaps, tiles, tile, width), bf16),
        in_specs=[pl.BlockSpec(memory_space=pltpu.HBM)] * 10,
        out_specs=pl.BlockSpec(memory_space=pl.ANY),
        scratch_shapes=[pltpu.VMEM((snaps, verts * tiles, tile, width), bf16)] * layers + [
            pltpu.VMEM((snaps, tiles, picks, tile, tile), jnp.int32),
            pltpu.VMEM((snaps, tiles, tile, picks * tile), bf16),
            pltpu.VMEM((layers, tiles, snaps, tile, width), bf16),
            pltpu.VMEM((layers, tiles, 2 * held, rows, width), bf16),
            pltpu.VMEM((layers, tiles, held, rows, width), bf16),
            pltpu.VMEM(graph_up.shape, bf16),
            pltpu.VMEM(graph_down.shape, bf16),
            pltpu.VMEM(time_up.shape, bf16),
            pltpu.VMEM(time_down.shape, bf16),
            dma,
            dma((4, layers)),
            dma((tiles,)),
            dma((verts - 1,)),
            dma((verts - 1,)),
            dma,
            dma((layers, tiles)),
            dma((layers, min(EARLY, tiles), group - 1)),
            dma((layers - 1, verts - 1)),
            dma((layers - 1, verts - 1)),
            dma,
            dma((layers, tiles)),
            dma,
            dma(((layers - 1) * tiles + 1,)),
            dma((layers - 1, verts - 1)),
            dma((layers - 1, verts - 1)),
            dma,
            pltpu.SMEM(tile_cols.shape, jnp.int32),
            pltpu.VMEM(graph_gain.shape, jnp.float32),
            pltpu.VMEM(lag_mix.shape, jnp.float32),
            pltpu.VMEM(time_gain.shape, jnp.float32),
            dma((4,)),
        ],
        compiler_params=pltpu.CompilerParams(
            collective_id=0, has_side_effects=True, vmem_limit_bytes=36 * 1024 * 1024
        ),
    )(
        *[pltpu.with_memory_space_constraint(array, pltpu.HBM) for array in (
            features.reshape(snaps, tiles, tile, width), tile_cols, tile_weights,
            graph_gain, lag_mix, time_gain, graph_up, graph_down, time_up, time_down,
        )]
    )
    return result.reshape(features.shape)


def solution(mesh):
    return jax.shard_map(
        functools.partial(on_device, mesh.shape["snap"], mesh.shape["vert"]),
        mesh=mesh,
        in_specs=(
            P("snap", "vert", None),
            P("snap", "vert", None),
            P("snap", "vert", None, None, None),
        ) + (P(),) * 7,
        out_specs=P("snap", "vert", None),
        check_vma=False,
    )
```

time: 43.3 us -> 41.8 us (0.965)
  Pallas kernels: 42.1 us -> 40.8 us
    pallas_call x1, Pallas kernels: 42.1 us -> 40.8 us  [on_device(): pl.pallas_call(functools.partial(kernel, owners, verts, group), out_shape...]
where the time goes in v2:
time: 41.8 us; the launch traced here: 41.6 us
  Pallas kernels  40.8 us (98%)
  local copies, waits for them, and re-layouts  0.8 us (2%)
    pallas_call x1, Pallas kernels, on_device(): pl.pallas_call(functools.partial(kernel, owners, verts, group), out_shape...  40.8 us

profile of v2, /device:TPU:16, one launch (start us, length us, event | category | flops | bytes accessed | tf_op | source)
XLA Modules:
  0.0 41.6 jit_solution(13040469940623690950)
XLA Ops:
  0.0 40.8 %shard_map.100 = bf16[2,8,128,128]{3,2,1,0:T(8,128)(2,1)S(1)} custom-call(bf16[2,8,128,128]{3,2,1,0:T(8,128)(2,1)} %bitcast.3, s32[2,8,8]{2,1,0:T(8,128)} %cols_far.1, s32[2,8,8,128,128]{4,3,2,1,0:T(8,128)} %weights.1, f32[2,128]{1,0:T(2,128)} %graph_gain_far.1, f32[2,8,128]{2,1,0:T(8,128)} %lag_mix_far.1, f32[2,128]{1,0:T(2,128)} %time_gain_far.1, ...), custom_call_target="tpu_custom_call" | custom-call | tf_op jit(solution)/shard_map/pallas_call | solution.py:386
  40.8 0.8 %copy.12 = bf16[2,1024,128]{2,1,0:T(8,128)(2,1)} copy(bf16[2,1024,128]{2,1,0:T(8,128)(2,1)S(1)} %bitcast.2) | data formatting | bytes 1048576

commit v3 on v2

--- a/solution.py
+++ b/solution.py
@@ -11,6 +11,10 @@
 MESH = pl.DeviceIdType.MESH
 STRIP = 16
 EARLY = 3
+SOONER = 8
+CROSSING = 2
+FIRST_CROSSING = 5
+SIDEWAYS = 1
 BEHIND = 4
 
 
@@ -33,9 +37,10 @@
     layers = lag_mix_far.shape[0]
     full = scratch[:layers]
     (
-        raw, blocks, sent_graph, window, sent_time,
+        raw, blocks, sent_graph, window, sent_time, near, part_out, part_in, near_done,
         graph_up, graph_down, time_up, time_down, own_sem, far_sem, raw_sem, first_send, first_recv,
-        a_send, a_recv, a_soon, cross_send, cross_recv, z_send, z_recv, b_send, b_recv, v_send, v_recv, out_sem,
+        a_send, a_recv, cross_send, cross_recv, z_send, z_recv, b_send, b_recv, v_send, v_recv, out_sem,
+        nz_send, nz_recv, ny_send, ny_recv, nx_send, nx_recv, near_sem,
         cols, graph_gain, lag_mix, time_gain, small_sem,
     ) = scratch[layers:]
     snaps, tiles, tile, width = feats.shape
@@ -45,7 +50,11 @@
     held = group * snaps
     unused = held - (lags - 1)
     groups = owners // group
-    early = min(EARLY, tiles)
+    near_tiles = near_list(group, tiles)
+    far_tiles = [r for r in range(tiles) if r not in near_tiles]
+    apart, count = len(far_tiles), len(near_tiles)
+    early = min(EARLY, apart)
+    sooner = min(SOONER, apart)
     skip = min(unused, snaps - 1)
 
     me = lax.axis_index("snap")
@@ -54,6 +63,7 @@
     plane = me // group
     base = me - slot
     first_tile = core * tiles
+    slot_x, slot_y = slot % 2, slot // 2
 
     def partner(d, back=False):
         if group == 4:
@@ -63,14 +73,19 @@
     def strip(owner):
         return pl.ds(pl.multiple_of(owner * rows, rows), rows)
 
-    def far_copy(i, l):
-        far, near = (
+    far_copies = [
+        pltpu.make_async_copy(far, near, far_sem.at[i])
+        for i, (far, near) in enumerate([
             (graph_up_far, graph_up), (graph_down_far, graph_down), (time_up_far, time_up), (time_down_far, time_down)
-        )[i]
-        return pltpu.make_async_copy(far.at[l], near.at[l], far_sem.at[i, l])
-
-    def raw_copy(r):
-        return pltpu.make_async_copy(weights.at[:, r], raw.at[:, r], raw_sem.at[r])
+        ])
+    ]
+    loads = [(r, 1) for r in range(min(2, tiles))]
+    while sum(loads[-1]) < tiles:
+        loads.append((sum(loads[-1]), min(2, tiles - sum(loads[-1]))))
+
+    def raw_copy(i):
+        span = pl.ds(*loads[i])
+        return pltpu.make_async_copy(weights.at[:, span], raw.at[:, span], raw_sem.at[i])
 
     smalls = [
         pltpu.make_async_copy(src, dst, small_sem.at[i])
@@ -98,17 +113,18 @@
     own_copy.start()
     for copy in smalls:
         copy.start()
-    soon = min(2, tiles)
-    for r in range(soon):
-        raw_copy(r).start()
+    for i in range(min(2, tiles)):
+        raw_copy(i).start()
     for i in range(2):
-        far_copy(i, 0).start()
+        far_copies[i].start()
 
     @pl.when(plane == 0)
     def _():
         for l in range(layers):
-            for w in range(tiles):
+            for w in range(apart):
                 window[l, w, 0:held] = jnp.zeros((held, rows, width), jnp.bfloat16)
+            for n in range(count):
+                near[l, n, 0:snaps] = jnp.zeros((snaps, tile, width), jnp.bfloat16)
 
     ahead = jnp.where(plane < groups - 1, 1, 0)
     behind = jnp.where(plane > 0, 1, 0)
@@ -127,15 +143,15 @@
 
     for q in range(1, verts):
         first_copy(q).start()
-    for r in range(soon, tiles):
-        raw_copy(r).start()
-    for l in range(layers):
-        for i in range(4):
-            if l > 0 or i > 1:
-                far_copy(i, l).start()
+    for i in range(min(2, tiles), len(loads)):
+        raw_copy(i).start()
+    for i in range(2, 4):
+        far_copies[i].start()
 
     def convert(r):
-        raw_copy(r).wait()
+        for i, (first, _) in enumerate(loads):
+            if first == r:
+                raw_copy(i).wait()
         for t in range(snaps):
             blocks[t, r] = jnp.concatenate(
                 [raw[t, r, k].astype(jnp.float32).astype(jnp.bfloat16) for k in range(picks)], axis=1
@@ -160,17 +176,19 @@
     onward = (jnp.minimum(me + group, owners - 1), core)
     others = (group - 1) * snaps
 
+    def a_mark(w, d):
+        return 2 * w + (1 if d == group - 1 else 0) if w < early else w + early
+
     def a_copy(l, w, d):
         owner = partner(d)
-        arrived = a_soon.at[l, w, d - 1] if w < early else a_recv.at[l, w]
         return remote(
             sent_graph.at[l, w, :, strip(owner)], window.at[l, w, pl.ds(held + slot * snaps, snaps)],
-            a_send, arrived, (base + owner, core),
-        )
-
-    def a_all(l, w):
-        part = window.at[l, w, pl.ds(0, others)]
-        return remote(part, part, a_send, a_recv.at[l, w], beside)
+            a_send, a_recv.at[a_mark(w, d)], (base + owner, core),
+        )
+
+    def a_some(l, w, count, d):
+        part = window.at[l, w, pl.ds(0, count * snaps)]
+        return remote(part, part, a_send, a_recv.at[a_mark(w, d)], beside)
 
     def z_copy(l, w, start, count):
         return remote(
@@ -195,10 +213,11 @@
             z_copy(l, w, origin * snaps, snaps).start()
 
     def b_mark(l, w):
-        return l * tiles + w if l < layers - 1 else (layers - 1) * tiles
+        return l * apart + w if l < layers - 1 else (layers - 1) * apart
 
     def target(l, w):
-        place = out.at[:, w] if l == layers - 1 else full[l + 1].at[:, first_tile + w]
+        r = far_tiles[w]
+        place = out.at[:, r] if l == layers - 1 else full[l + 1].at[:, first_tile + r]
         return place.at[:, strip(slot)]
 
     def b_copy(l, w, d):
@@ -211,7 +230,7 @@
     def cross_copy(l, d, q):
         home = partner(d)
         return remote(
-            sent_time.at[l, tiles - 1, pl.ds(home * snaps, snaps)], target(l, tiles - 1),
+            sent_time.at[l, apart - 1, pl.ds(home * snaps, snaps)], target(l, apart - 1),
             cross_send.at[l, q - 1], cross_recv.at[l, q - 1], (base + home, (core + q) % verts),
         )
 
@@ -225,7 +244,7 @@
 
     def out_copy(w):
         own = sent_time.at[layers - 1, w, pl.ds(slot * snaps, snaps)]
-        return pltpu.make_async_copy(own, out.at[:, w, strip(slot)], out_sem)
+        return pltpu.make_async_copy(own, out.at[:, far_tiles[w], strip(slot)], out_sem)
 
     def v_copy(l, part, q):
         return remote(part, part, v_send.at[l, q - 1], v_recv.at[l, q - 1], (me, (core + q) % verts))
@@ -236,6 +255,104 @@
     def v_start(l, r):
         for q in range(1, verts):
             v_copy(l, full[l + 1].at[:, first_tile + r], q).start()
+
+    def nz_copy(l, n, first):
+        return remote(
+            near.at[l, n, pl.ds(2 * snaps + first, snaps - first)], near.at[l, n, pl.ds(first, snaps - first)],
+            nz_send, nz_recv.at[l, n], onward,
+        )
+
+    def nz_do(act):
+        if skip == 0:
+            act(0)
+            return
+
+        @pl.when(slot == 0)
+        def _():
+            act(skip)
+
+        @pl.when(slot > 0)
+        def _():
+            act(0)
+
+    def ny_copy(l, n):
+        return remote(
+            near.at[l, n, pl.ds(2 * snaps * (1 - slot_y), snaps)], near.at[l, n, pl.ds(snaps, snaps)],
+            ny_send, ny_recv.at[l, n], (base + (slot + 2) % group, core),
+        )
+
+    def nx_copy(l, n):
+        return remote(
+            part_out.at[l, n], part_in.at[l, n], nx_send, nx_recv.at[l, n], (base + slot + 1 - 2 * slot_x, core)
+        )
+
+    def lag_sum(l, i, sources):
+        total = None
+        for apart_by, values in sources:
+            for j in range(snaps):
+                lag = apart_by * snaps + i - j
+                if 0 <= lag < lags:
+                    term = lag_mix[l, lag:lag + 1] * values[j]
+                    total = term if total is None else total + term
+        return total
+
+    def near_load(l, n, first, span):
+        return [near[l, n, first + j, span].astype(jnp.float32) for j in range(snaps)]
+
+    def near_y(l, n):
+        @pl.when(slot_y == 1)
+        def _():
+            @pl.when(plane > 0)
+            def _():
+                nz_do(lambda first: nz_copy(l, n, first).wait_recv())
+
+            ny_copy(l, n).start()
+
+        @pl.when(slot_y == 0)
+        def _():
+            ny_copy(l, n).start()
+
+    def near_x(l, n):
+        @pl.when((slot_y == 0) & (plane > 0))
+        def _():
+            nz_do(lambda first: nz_copy(l, n, first).wait_recv())
+
+        ny_copy(l, n).wait_recv()
+        for top in range(0, tile, STRIP):
+            span = slice(top, top + STRIP)
+            newer = near_load(l, n, snaps * (2 - slot_x), span)
+            older = near_load(l, n, snaps * (1 - slot_x), span)
+            for i in range(snaps):
+                part_out[l, n, i, span] = lag_sum(l, i, [(1, newer), (3, older)]).astype(jnp.bfloat16)
+        nx_copy(l, n).start()
+
+    def near_time(l, n):
+        r = near_tiles[n]
+        nx_copy(l, n).wait_recv()
+        spots, mixes, states = [], [], []
+        for top in range(0, tile, STRIP):
+            span = slice(top, top + STRIP)
+            seen = [near_load(l, n, snaps * p, span) for p in range(3)]
+            for i in range(snaps):
+                mixed = lag_sum(l, i, [(0, seen[2]), (2, seen[1]), (4, seen[0])])
+                mixes.append(mixed + part_in[l, n, i, span].astype(jnp.float32))
+                states.append(seen[2][i])
+                spots.append((i, span))
+        branch = mlp(normalise(jnp.concatenate(mixes, axis=0), time_gain[l:l + 1]), time_up[l], time_down[l])
+        result = (jnp.concatenate(states, axis=0) + branch).astype(jnp.bfloat16)
+        for k, (i, span) in enumerate(spots):
+            piece = result[k * STRIP:(k + 1) * STRIP]
+            if l == layers - 1:
+                near_done[n, i, span] = piece
+            else:
+                full[l + 1][i, first_tile + r, span] = piece
+        if l == layers - 1:
+            near_out(n).start()
+        else:
+            v_start(l, r)
+
+    def near_out(n):
+        return pltpu.make_async_copy(near_done.at[n], out.at[:, near_tiles[n]], near_sem)
 
     def graph_step(l, r):
         if l == 0 and r > 0:
@@ -248,26 +365,37 @@
         branch = mlp(normalise(summed, graph_gain[l:l + 1]), graph_up[l], graph_down[l])
         state = full[l][:, first_tile + r].astype(jnp.float32)
         result = (state + branch.reshape(snaps, tile, width)).astype(jnp.bfloat16)
-        sent_graph[l, r] = result
-        for d in range(1, group):
-            a_copy(l, r, d).start()
-        window[l, r, pl.ds(held + slot * snaps, snaps)] = sent_graph[l, r, :, strip(slot)]
+        if r in near_tiles:
+            n = near_tiles.index(r)
+            near[l, n, 2 * snaps:3 * snaps] = result
+
+            @pl.when(plane < groups - 1)
+            def _():
+                nz_do(lambda first: nz_copy(l, n, first).start())
+
+            return
+        w = far_tiles.index(r)
+        sent_graph[l, w] = result
+        for d in range(1, group) if w < early else reversed(range(1, group)):
+            a_copy(l, w, d).start()
+        window[l, w, pl.ds(held + slot * snaps, snaps)] = sent_graph[l, w, :, strip(slot)]
+
+        if w < sooner:
+
+            @pl.when(plane < groups - 1)
+            def _():
+                z_origin(l, w, slot)
+
+    def forward(l, w, parts):
+        a_some(l, w, len(parts), parts[-1]).wait_recv()
 
         @pl.when(plane < groups - 1)
         def _():
-            z_origin(l, r, slot)
-
-    def forward(l, w, parts):
-        if w >= early:
-            a_all(l, w).wait_recv()
-        else:
-            for d in parts:
-                a_copy(l, w, d).wait_recv()
-
-        @pl.when(plane < groups - 1)
-        def _():
-            for d in parts:
-                z_origin(l, w, partner(d, True))
+            if w < sooner:
+                for d in parts:
+                    z_origin(l, w, partner(d, True))
+            else:
+                z_all(l, w).start()
 
     def forward_most(l, w):
         forward(l, w, range(1, group - 1))
@@ -298,51 +426,70 @@
         result = (jnp.concatenate(states, axis=0) + branch).astype(jnp.bfloat16)
         for n, (i, span) in enumerate(spots):
             sent_time[l, w, i, span] = result[n * STRIP:(n + 1) * STRIP]
-        for d in range(1, group):
+        for d in reversed(range(1, group)):
             b_copy(l, w, d).start()
-        if l < layers - 1 and w == tiles - 1:
+            if l < layers - 1 and w == apart - 1:
+                for q in range(1, verts):
+                    cross_copy(l, d, q).start()
+        if l < layers - 1 and w == apart - 1:
             for q in range(1, verts):
-                for d in range(group):
-                    cross_copy(l, d, q).start()
+                cross_copy(l, 0, q).start()
         if l == layers - 1:
             out_copy(w).start()
         else:
             own = sent_time[l, w, pl.ds(slot * snaps, snaps)]
-            full[l + 1][:, first_tile + w, strip(slot)] = own
+            full[l + 1][:, first_tile + far_tiles[w], strip(slot)] = own
 
     def collect(l, w):
         b_all(l, w).wait_recv()
-        if w < tiles - 1:
-            v_start(l, w)
+        if w < apart - 1:
+            v_start(l, far_tiles[w])
 
     def run(kind, step, l, n):
         with jax.named_scope(f"{kind}{l}_{n}"):
             step(l, n)
 
     for l in range(layers):
-        for i in range(2):
-            far_copy(i, l).wait()
+        if l == 0:
+            for i in range(2):
+                far_copies[i].wait()
+        ready = {}
+        for w in range(early):
+            ready.setdefault(min(far_tiles[w] + BEHIND + 1, tiles - 1), []).append(("fl", forward_last, w))
+            ready.setdefault(min(far_tiles[w] + BEHIND, tiles - 1), []).append(("fm", forward_most, w))
         for r in range(tiles):
             run("g", graph_step, l, r)
-            w = r - BEHIND
-            if 1 <= w <= early:
-                run("fl", forward_last, l, w - 1)
-            if 0 <= w < early:
-                run("fm", forward_most, l, w)
-        for i in range(2, 4):
-            far_copy(i, l).wait()
-        for w in range(max(tiles - BEHIND, 0), early):
-            run("fm", forward_most, l, w)
-        for w in range(max(tiles - BEHIND - 1, 0), early):
-            run("fl", forward_last, l, w)
+            if r == tiles - SIDEWAYS:
+                for n in range(count):
+                    run("y", near_y, l, n)
+            for kind, step, w in sorted(ready.get(r, []), key=lambda item: (item[2], item[0] == "fl")):
+                run(kind, step, l, w)
+        if l == 0:
+            for i in range(2, 4):
+                far_copies[i].wait()
         passed = early
-        for w in range(tiles):
-            while passed < min(w + BEHIND, tiles):
+        for w in range(apart):
+            while passed < min(w + BEHIND, apart):
                 run("f", forward_all, l, passed)
                 passed += 1
             run("t", time_step, l, w)
+            for n in range(count):
+                if w == min(CROSSING, apart - 1):
+
+                    @pl.when(plane > 0)
+                    def _():
+                        run("x", near_x, l, n)
+
+                if w == min(FIRST_CROSSING, apart - 1):
+
+                    @pl.when(plane == 0)
+                    def _():
+                        run("x", near_x, l, n)
+
+        for n in range(count):
+            run("n", near_time, l, n)
         if l < layers - 1:
-            for w in range(tiles):
+            for w in range(apart):
                 run("c", collect, l, w)
             with jax.named_scope(f"v{l}"):
                 for q in range(1, verts):
@@ -355,10 +502,10 @@
     with jax.named_scope("drain"):
         for q in range(1, verts):
             first_copy(q).wait_send()
-        part = out.at[:, :, pl.ds(0, rows)]
+        part = out.at[:, pl.ds(0, apart), pl.ds(0, rows)]
         pltpu.make_async_copy(part, part, out_sem).wait()
         part = window.at[:, :, pl.ds(0, others)]
-        remote(part, part, a_send, a_recv.at[0, 0], beside).wait_send()
+        remote(part, part, a_send, a_recv.at[0], beside).wait_send()
         part = sent_time.at[:, :, pl.ds(0, others)]
         remote(part, part, b_send, b_recv.at[0], beside).wait_send()
         for l in range(layers - 1):
@@ -370,6 +517,25 @@
         def _():
             part = window.at[:, :, pl.ds(unused, held - unused)]
             remote(part, part, z_send, z_recv.at[0, 0], onward).wait_send()
+
+        if count > 0:
+            part = out.at[:, pl.ds(0, count)]
+            pltpu.make_async_copy(part, part, near_sem).wait()
+            part = near.at[:, :, pl.ds(0, snaps)]
+            remote(part, part, ny_send, ny_recv.at[0, 0], beside).wait_send()
+            remote(part_out, part_out, nx_send, nx_recv.at[0, 0], beside).wait_send()
+
+            @pl.when(plane < groups - 1)
+            def _():
+                def take(first):
+                    part = near.at[:, :, pl.ds(first, snaps - first)]
+                    remote(part, part, nz_send, nz_recv.at[0, 0], onward).wait_send()
+
+                nz_do(take)
+
+
+def near_list(group, tiles):
+    return [1] if group == 4 and tiles > 4 else []
 
 
 def on_device(owners, verts, features, tile_cols, tile_weights, graph_gain, graph_up, graph_down, lag_mix, time_gain, time_up, time_down):
@@ -381,6 +547,8 @@
         group += 1
     rows = tile // group
     held = group * snaps
+    near_count = len(near_list(group, tiles))
+    apart, count = tiles - near_count, max(near_count, 1)
     bf16 = jnp.bfloat16
     dma = pltpu.SemaphoreType.DMA
     result = pl.pallas_call(
@@ -391,29 +559,34 @@
         scratch_shapes=[pltpu.VMEM((snaps, verts * tiles, tile, width), bf16)] * layers + [
             pltpu.VMEM((snaps, tiles, picks, tile, tile), jnp.int32),
             pltpu.VMEM((snaps, tiles, tile, picks * tile), bf16),
-            pltpu.VMEM((layers, tiles, snaps, tile, width), bf16),
-            pltpu.VMEM((layers, tiles, 2 * held, rows, width), bf16),
-            pltpu.VMEM((layers, tiles, held, rows, width), bf16),
+            pltpu.VMEM((layers, apart, snaps, tile, width), bf16),
+            pltpu.VMEM((layers, apart, 2 * held, rows, width), bf16),
+            pltpu.VMEM((layers, apart, held, rows, width), bf16),
+            pltpu.VMEM((layers, count, 3 * snaps, tile, width), bf16),
+            pltpu.VMEM((layers, count, snaps, tile, width), bf16),
+            pltpu.VMEM((layers, count, snaps, tile, width), bf16),
+            pltpu.VMEM((count, snaps, tile, width), bf16),
             pltpu.VMEM(graph_up.shape, bf16),
             pltpu.VMEM(graph_down.shape, bf16),
             pltpu.VMEM(time_up.shape, bf16),
             pltpu.VMEM(time_down.shape, bf16),
             dma,
-            dma((4, layers)),
+            dma((4,)),
             dma((tiles,)),
             dma((verts - 1,)),
             dma((verts - 1,)),
             dma,
-            dma((layers, tiles)),
-            dma((layers, min(EARLY, tiles), group - 1)),
+            dma((apart + min(EARLY, apart),)),
             dma((layers - 1, verts - 1)),
             dma((layers - 1, verts - 1)),
             dma,
-            dma((layers, tiles)),
+            dma((layers, apart)),
             dma,
-            dma(((layers - 1) * tiles + 1,)),
+            dma(((layers - 1) * apart + 1,)),
             dma((layers - 1, verts - 1)),
             dma((layers - 1, verts - 1)),
+            dma,
+        ] + [dma, dma((layers, count))] * 3 + [
             dma,
             pltpu.SMEM(tile_cols.shape, jnp.int32),
             pltpu.VMEM(graph_gain.shape, jnp.float32),

time: 41.8 us -> 40.5 us (0.969)
  Pallas kernels: 40.8 us -> 39.6 us
    pallas_call x1, Pallas kernels: 40.8 us -> 39.6 us  [on_device(): pl.pallas_call(functools.partial(kernel, owners, verts, group), out_shape...]
where the time goes in v3:
time: 40.5 us; the launch traced here: 40.4 us
  Pallas kernels  39.6 us (98%)
  local copies, waits for them, and re-layouts  0.8 us (2%)
    pallas_call x1, Pallas kernels, on_device(): pl.pallas_call(functools.partial(kernel, owners, verts, group), out_shape...  39.6 us

profile of v3, /device:TPU:16, one launch (start us, length us, event | category | flops | bytes accessed | tf_op | source)
XLA Modules:
  0.0 40.4 jit_solution(11075108402360593120)
XLA Ops:
  0.0 39.6 %shard_map.100 = bf16[2,8,128,128]{3,2,1,0:T(8,128)(2,1)S(1)} custom-call(bf16[2,8,128,128]{3,2,1,0:T(8,128)(2,1)} %bitcast.3, s32[2,8,8]{2,1,0:T(8,128)} %cols_far.1, s32[2,8,8,128,128]{4,3,2,1,0:T(8,128)} %weights.1, f32[2,128]{1,0:T(2,128)} %graph_gain_far.1, f32[2,8,128]{2,1,0:T(8,128)} %lag_mix_far.1, f32[2,128]{1,0:T(2,128)} %time_gain_far.1, ...), custom_call_target="tpu_custom_call" | custom-call | tf_op jit(solution)/shard_map/pallas_call | solution.py:554
  39.6 0.8 %copy.12 = bf16[2,1024,128]{2,1,0:T(8,128)(2,1)} copy(bf16[2,1024,128]{2,1,0:T(8,128)(2,1)S(1)} %bitcast.2) | data formatting | bytes 1048576

commit v4 on v3

--- a/solution.py
+++ b/solution.py
@@ -10,10 +10,12 @@
 eps = 1e-06
 MESH = pl.DeviceIdType.MESH
 STRIP = 16
+GELU_A = 0.7978845608028654
+GELU_B = GELU_A * 0.044715
 EARLY = 3
 SOONER = 8
 CROSSING = 2
-FIRST_CROSSING = 5
+FIRST_CROSSING = 4
 SIDEWAYS = 1
 BEHIND = 4
 
@@ -25,7 +27,10 @@
 
 def mlp(normed, up_weight, down_weight):
     hidden = jnp.dot(normed, up_weight, preferred_element_type=jnp.float32)
-    hidden = jax.nn.gelu(hidden.astype(jnp.bfloat16))
+    hidden = hidden.astype(jnp.bfloat16)
+    inner = hidden * (GELU_A + GELU_B * (hidden * hidden))
+    half = hidden * 0.5
+    hidden = half + half * jnp.tanh(inner)
     return jnp.dot(hidden, down_weight, preferred_element_type=jnp.float32)
 
 
@@ -39,7 +44,7 @@
     (
         raw, blocks, sent_graph, window, sent_time, near, part_out, part_in, near_done,
         graph_up, graph_down, time_up, time_down, own_sem, far_sem, raw_sem, first_send, first_recv,
-        a_send, a_recv, cross_send, cross_recv, z_send, z_recv, b_send, b_recv, v_send, v_recv, out_sem,
+        a_send, a_recv, cross_send, cross_recv, z_send, z_recv, z_late, b_send, b_recv, v_send, v_recv, out_sem,
         nz_send, nz_recv, ny_send, ny_recv, nx_send, nx_recv, near_sem,
         cols, graph_gain, lag_mix, time_gain, small_sem,
     ) = scratch[layers:]
@@ -54,7 +59,8 @@
     far_tiles = [r for r in range(tiles) if r not in near_tiles]
     apart, count = len(far_tiles), len(near_tiles)
     early = min(EARLY, apart)
-    sooner = min(SOONER, apart)
+    halved = [apart - 1] if rows % (2 * STRIP) == 0 and apart > early else []
+    sooner = min(SOONER, apart - len(halved))
     skip = min(unused, snaps - 1)
 
     me = lax.axis_index("snap")
@@ -113,10 +119,7 @@
     own_copy.start()
     for copy in smalls:
         copy.start()
-    for i in range(min(2, tiles)):
-        raw_copy(i).start()
-    for i in range(2):
-        far_copies[i].start()
+    raw_copy(0).start()
 
     @pl.when(plane == 0)
     def _():
@@ -143,7 +146,9 @@
 
     for q in range(1, verts):
         first_copy(q).start()
-    for i in range(min(2, tiles), len(loads)):
+    for i in range(2):
+        far_copies[i].start()
+    for i in range(1, len(loads)):
         raw_copy(i).start()
     for i in range(2, 4):
         far_copies[i].start()
@@ -199,6 +204,14 @@
     def z_all(l, w):
         return z_copy(l, w, unused, held - unused)
 
+    def z_half(l, w, half):
+        span = pl.ds(half * (rows // 2), rows // 2)
+        arrived = z_recv.at[l, w] if half == 0 else z_late.at[l]
+        return remote(
+            window.at[l, w, pl.ds(held + unused, held - unused), span],
+            window.at[l, w, pl.ds(unused, held - unused), span], z_send, arrived, onward,
+        )
+
     def z_origin(l, w, origin):
         if unused == 0:
             z_copy(l, w, origin * snaps, snaps).start()
@@ -215,22 +228,22 @@
     def b_mark(l, w):
         return l * apart + w if l < layers - 1 else (layers - 1) * apart
 
-    def target(l, w):
+    def target(l, w, top, size):
         r = far_tiles[w]
         place = out.at[:, r] if l == layers - 1 else full[l + 1].at[:, first_tile + r]
-        return place.at[:, strip(slot)]
-
-    def b_copy(l, w, d):
+        return place.at[:, pl.ds(pl.multiple_of(slot * rows + top, STRIP), size)]
+
+    def b_copy(l, w, d, top, size):
         home = partner(d)
         return remote(
-            sent_time.at[l, w, pl.ds(home * snaps, snaps)], target(l, w),
+            sent_time.at[l, w, pl.ds(home * snaps, snaps), pl.ds(top, size)], target(l, w, top, size),
             b_send, b_recv.at[b_mark(l, w)], (base + home, core),
         )
 
-    def cross_copy(l, d, q):
+    def cross_copy(l, d, q, top, size):
         home = partner(d)
         return remote(
-            sent_time.at[l, apart - 1, pl.ds(home * snaps, snaps)], target(l, apart - 1),
+            sent_time.at[l, apart - 1, pl.ds(home * snaps, snaps), pl.ds(top, size)], target(l, apart - 1, top, size),
             cross_send.at[l, q - 1], cross_recv.at[l, q - 1], (base + home, (core + q) % verts),
         )
 
@@ -242,9 +255,9 @@
         part = sent_time.at[l, w, pl.ds(0, others)] if l < layers - 1 else sent_time.at[l, :, pl.ds(0, others)]
         return remote(part, part, b_send, b_recv.at[b_mark(l, w)], beside)
 
-    def out_copy(w):
-        own = sent_time.at[layers - 1, w, pl.ds(slot * snaps, snaps)]
-        return pltpu.make_async_copy(own, out.at[:, far_tiles[w], strip(slot)], out_sem)
+    def out_copy(w, top, size):
+        own = sent_time.at[layers - 1, w, pl.ds(slot * snaps, snaps), pl.ds(top, size)]
+        return pltpu.make_async_copy(own, target(layers - 1, w, top, size), out_sem)
 
     def v_copy(l, part, q):
         return remote(part, part, v_send.at[l, q - 1], v_recv.at[l, q - 1], (me, (core + q) % verts))
@@ -394,6 +407,9 @@
             if w < sooner:
                 for d in parts:
                     z_origin(l, w, partner(d, True))
+            elif w in halved:
+                z_half(l, w, 0).start()
+                z_half(l, w, 1).start()
             else:
                 z_all(l, w).start()
 
@@ -411,8 +427,18 @@
         def _():
             z_all(l, w).wait_recv()
 
+        time_rows(l, w, 0, rows)
+
+    def time_half(l, w, half):
+        @pl.when(plane > 0)
+        def _():
+            z_half(l, w, half).wait_recv()
+
+        time_rows(l, w, half * (rows // 2), rows // 2)
+
+    def time_rows(l, w, start, size):
         spots, mixes, states = [], [], []
-        for top in range(0, rows, STRIP):
+        for top in range(start, start + size, STRIP):
             span = slice(top, top + STRIP)
             seen = {i: window[l, w, i, span].astype(jnp.float32) for i in range(unused, 2 * held)}
             for i in range(held):
@@ -426,19 +452,21 @@
         result = (jnp.concatenate(states, axis=0) + branch).astype(jnp.bfloat16)
         for n, (i, span) in enumerate(spots):
             sent_time[l, w, i, span] = result[n * STRIP:(n + 1) * STRIP]
+        crossing = l < layers - 1 and w == apart - 1
         for d in reversed(range(1, group)):
-            b_copy(l, w, d).start()
-            if l < layers - 1 and w == apart - 1:
+            b_copy(l, w, d, start, size).start()
+            if crossing:
                 for q in range(1, verts):
-                    cross_copy(l, d, q).start()
-        if l < layers - 1 and w == apart - 1:
+                    cross_copy(l, d, q, start, size).start()
+        if crossing:
             for q in range(1, verts):
-                cross_copy(l, 0, q).start()
+                cross_copy(l, 0, q, start, size).start()
         if l == layers - 1:
-            out_copy(w).start()
+            out_copy(w, start, size).start()
         else:
-            own = sent_time[l, w, pl.ds(slot * snaps, snaps)]
-            full[l + 1][:, first_tile + far_tiles[w], strip(slot)] = own
+            own = sent_time[l, w, pl.ds(slot * snaps, snaps), start:start + size]
+            place = pl.ds(pl.multiple_of(slot * rows + start, STRIP), size)
+            full[l + 1][:, first_tile + far_tiles[w], place] = own
 
     def collect(l, w):
         b_all(l, w).wait_recv()
@@ -472,17 +500,22 @@
             while passed < min(w + BEHIND, apart):
                 run("f", forward_all, l, passed)
                 passed += 1
-            run("t", time_step, l, w)
+            if w in halved:
+                for half in range(2):
+                    with jax.named_scope(f"t{l}_{w}_{half}"):
+                        time_half(l, w, half)
+            else:
+                run("t", time_step, l, w)
             for n in range(count):
-                if w == min(CROSSING, apart - 1):
-
-                    @pl.when(plane > 0)
+                if w == min(CROSSING + l, apart - 1):
+
+                    @pl.when(plane > l)
                     def _():
                         run("x", near_x, l, n)
 
                 if w == min(FIRST_CROSSING, apart - 1):
 
-                    @pl.when(plane == 0)
+                    @pl.when(plane <= l)
                     def _():
                         run("x", near_x, l, n)
 
@@ -572,7 +605,7 @@
             pltpu.VMEM(time_down.shape, bf16),
             dma,
             dma((4,)),
-            dma((tiles,)),
+            dma((tiles // 2 + 1,)),
             dma((verts - 1,)),
             dma((verts - 1,)),
             dma,
@@ -581,6 +614,7 @@
             dma((layers - 1, verts - 1)),
             dma,
             dma((layers, apart)),
+            dma((layers,)),
             dma,
             dma(((layers - 1) * apart + 1,)),
             dma((layers - 1, verts - 1)),

time: 40.5 us -> 40.3 us (level)
  no operation moved by 1% of the time
where the time goes in v4:
time: 40.3 us; the launch traced here: 40.2 us
  Pallas kernels  39.4 us (98%)
  local copies, waits for them, and re-layouts  0.8 us (2%)
    pallas_call x1, Pallas kernels, on_device(): pl.pallas_call(functools.partial(kernel, owners, verts, group), out_shape...  39.4 us

profile of v4, /device:TPU:16, one launch (start us, length us, event | category | flops | bytes accessed | tf_op | source)
XLA Modules:
  0.0 40.2 jit_solution(14575926718260441484)
XLA Ops:
  0.0 39.4 %shard_map.100 = bf16[2,8,128,128]{3,2,1,0:T(8,128)(2,1)S(1)} custom-call(bf16[2,8,128,128]{3,2,1,0:T(8,128)(2,1)} %bitcast.3, s32[2,8,8]{2,1,0:T(8,128)} %cols_far.1, s32[2,8,8,128,128]{4,3,2,1,0:T(8,128)} %weights.1, f32[2,128]{1,0:T(2,128)} %graph_gain_far.1, f32[2,8,128]{2,1,0:T(8,128)} %lag_mix_far.1, f32[2,128]{1,0:T(2,128)} %time_gain_far.1, ...), custom_call_target="tpu_custom_call" | custom-call | tf_op jit(solution)/shard_map/pallas_call | solution.py:587
  39.4 0.8 %copy.12 = bf16[2,1024,128]{2,1,0:T(8,128)(2,1)} copy(bf16[2,1024,128]{2,1,0:T(8,128)(2,1)S(1)} %bitcast.2) | data formatting | bytes 1048576

commit v5 on v4

--- a/solution.py
+++ b/solution.py
@@ -568,7 +568,7 @@
 
 
 def near_list(group, tiles):
-    return [1] if group == 4 and tiles > 4 else []
+    return [2] if group == 4 and tiles > 4 else []
 
 
 def on_device(owners, verts, features, tile_cols, tile_weights, graph_gain, graph_up, graph_down, lag_mix, time_gain, time_up, time_down):

time: 40.3 us -> 40.2 us (level)
  no operation moved by 1% of the time
where the time goes in v5:
time: 40.2 us; the launch traced here: 40 us
  Pallas kernels  39.2 us (98%)
  local copies, waits for them, and re-layouts  0.8 us (2%)
    pallas_call x1, Pallas kernels, on_device(): pl.pallas_call(functools.partial(kernel, owners, verts, group), out_shape...  39.2 us

profile of v5, /device:TPU:16, one launch (start us, length us, event | category | flops | bytes accessed | tf_op | source)
XLA Modules:
  0.0 40.0 jit_solution(5633297386343103605)
XLA Ops:
  0.0 39.2 %shard_map.100 = bf16[2,8,128,128]{3,2,1,0:T(8,128)(2,1)S(1)} custom-call(bf16[2,8,128,128]{3,2,1,0:T(8,128)(2,1)} %bitcast.3, s32[2,8,8]{2,1,0:T(8,128)} %cols_far.1, s32[2,8,8,128,128]{4,3,2,1,0:T(8,128)} %weights.1, f32[2,128]{1,0:T(2,128)} %graph_gain_far.1, f32[2,8,128]{2,1,0:T(8,128)} %lag_mix_far.1, f32[2,128]{1,0:T(2,128)} %time_gain_far.1, ...), custom_call_target="tpu_custom_call" | custom-call | tf_op jit(solution)/shard_map/pallas_call | solution.py:587
  39.2 0.8 %copy.12 = bf16[2,1024,128]{2,1,0:T(8,128)(2,1)} copy(bf16[2,1024,128]{2,1,0:T(8,128)(2,1)S(1)} %bitcast.2) | data formatting | bytes 1048576
